TPU v7x, 32 devices: a whole 2x2x4 slice. The times are simulated.
32 devices in a mesh: batch: 8 (over y, x, core), rows: 4 (over z).
Axes of the slice: x: 2, y: 2, z: 4, core: 2. Of those that a mesh axis runs over, the one named last changes fastest.
Arguments:
- atoms: bfloat16 [32, 256, 512], P('batch', 'rows'), may hold values from -6 to 6
- pair_bias: bfloat16 [32, 64, 256, 256], P('batch', None, 'rows'), may hold values from -6 to 6
- lengths: int32 [32], P('batch'), may hold values from 64 to 256, as said below
- first_gain: bfloat16 [512], replicated, may hold values from 0.099609375 to 1.8984375
- first_shift: bfloat16 [512], replicated, may hold values from -3 to 3
- query_weight: bfloat16 [512, 512], replicated, may hold values from -0.25 to 0.25
- query_bias: bfloat16 [512], replicated, may hold values from -3 to 3
- key_weight: bfloat16 [512, 512], replicated, may hold values from -0.25 to 0.25
- value_weight: bfloat16 [512, 512], replicated, may hold values from -0.25 to 0.25
- value_bias: bfloat16 [512], replicated, may hold values from -3 to 3
- out_weight: bfloat16 [512, 512], replicated, may hold values from -1 to 1
- out_bias: bfloat16 [512], replicated, may hold values from -3 to 3
- second_gain: bfloat16 [512], replicated, may hold values from 0.099609375 to 1.8984375
- second_shift: bfloat16 [512], replicated, may hold values from -3 to 3
- inner_weight: bfloat16 [512, 2048], replicated, may hold values from -0.25 to 0.25
- inner_bias: bfloat16 [2048], replicated, may hold values from -3 to 3
- outer_weight: bfloat16 [2048, 512], replicated, may hold values from -0.125 to 0.125
- outer_bias: bfloat16 [512], replicated, may hold values from -3 to 3
- atoms_cotangent: bfloat16 [32, 256, 512], P('batch', 'rows'), may hold values from -6 to 6
- pair_cotangent: bfloat16 [32, 64, 256, 256], P('batch', None, 'rows'), may hold values from -6 to 6
Outputs:
- atoms_out: bfloat16 [32, 256, 512], P('batch', 'rows')
- pair_out: bfloat16 [32, 64, 256, 256], P('batch', None, 'rows')
- atoms_grad: bfloat16 [32, 256, 512], P('batch', 'rows')
- pair_grad: bfloat16 [32, 64, 256, 256], P('batch', None, 'rows')
- first_gain_grad: float32 [512], P('batch')
- first_shift_grad: float32 [512], P('batch')
- query_weight_grad: float32 [512, 512], P('batch')
- query_bias_grad: float32 [512], P('batch')
- key_weight_grad: float32 [512, 512], P('batch')
- value_weight_grad: float32 [512, 512], P('batch')
- value_bias_grad: float32 [512], P('batch')
- out_weight_grad: float32 [512, 512], P('batch')
- out_bias_grad: float32 [512], P('batch')
- second_gain_grad: float32 [512], P('batch')
- second_shift_grad: float32 [512], P('batch')
- inner_weight_grad: float32 [512, 2048], P('batch')
- inner_bias_grad: float32 [2048], P('batch')
- outer_weight_grad: float32 [2048, 512], P('batch')
- outer_bias_grad: float32 [512], P('batch')
Inputs may be any that keep to these rules, and one draw needn't show every extreme that they name: Atoms at positions lengths[m] and beyond are padding and are masked as keys; of the 4 molecules at each index of batch, one (drawn from the seed) has exactly 256 atoms.
All inputs are finite; a program needn't handle non-finite values.
Results may differ from a plain program's by a relative error of at most 0.012.
Values may be sent and summed in bfloat16 or wider, within the bound.
No kernel may reach another device: no remote copies, remote signals or barrier semaphores. Data moves between devices by JAX's collectives and lax.ppermute only.
A program may use at most 128 MiB of HBM per device.

v0:
```python
from functools import partial
import jax
import jax.numpy as jnp
from jax import lax
from jax.sharding import PartitionSpec as P

EPSILON = 1e-05
MASKED = -1000000000.0


def norm_forward(values_in, gain, shift):
    centre = values_in - jnp.mean(values_in, -1, keepdims=True)
    inverse = lax.rsqrt(jnp.mean(centre * centre, -1, keepdims=True) + EPSILON)
    normed = centre * inverse
    return (normed * gain + shift, normed, inverse)


def norm_backward(upstream, normed, inverse, gain):
    scaled = upstream * gain
    result = inverse * (
        scaled
        - jnp.mean(scaled, -1, keepdims=True)
        - normed * jnp.mean(scaled * normed, -1, keepdims=True)
    )
    return (result, jnp.sum(upstream * normed, 0), jnp.sum(upstream, 0))


def across(left, right):
    return lax.dot_general(
        left, right, (((0,), (0,)), ((), ())), preferred_element_type=jnp.float32
    )


def against(left, right):
    return lax.dot_general(
        left, right, (((1,), (1,)), ((), ())), preferred_element_type=jnp.float32
    )


def column_sum(values_in):
    return jnp.sum(values_in.astype(jnp.float32), 0)


def project_keys(hidden_rows, key_weight, value_weight, value_bias):
    key_rows = jnp.dot(hidden_rows, key_weight, preferred_element_type=jnp.float32).astype(
        jnp.bfloat16
    )
    value_rows = (
        jnp.dot(hidden_rows, value_weight, preferred_element_type=jnp.float32)
        + value_bias.astype(jnp.float32)
    ).astype(jnp.bfloat16)
    return (key_rows, value_rows)


def scores_of(factor, query_rows, key_rows, pair_rows, length):
    scores = factor * jnp.einsum(
        "ihe,jhe->hij", query_rows, key_rows, preferred_element_type=jnp.float32
    )
    scores = scores + pair_rows.astype(jnp.float32)
    valid = lax.broadcasted_iota(jnp.int32, scores.shape, 2) < length
    return (scores, valid)


def attend_forward(factor, pieces):
    query_rows, key_rows, value_rows, pair_rows, length = pieces
    scores, valid = scores_of(factor, query_rows, key_rows, pair_rows, length)
    masked = jnp.where(valid, scores, MASKED)
    highest = jnp.max(masked, -1, keepdims=True)
    weights = jnp.exp(masked - highest)
    totals = jnp.sum(weights, -1, keepdims=True)
    low_probs = (weights / totals).astype(jnp.bfloat16)
    mixed_rows = jnp.einsum(
        "hij,jhe->ihe", low_probs, value_rows, preferred_element_type=jnp.float32
    )
    return (
        scores.astype(jnp.bfloat16),
        mixed_rows.astype(jnp.bfloat16),
        (highest + jnp.log(totals))[..., 0],
    )


def attend_backward(factor, pieces):
    query_rows, key_rows, value_rows, pair_rows, length, log_totals, mixed_grad, pair_cot = pieces
    scores, valid = scores_of(factor, query_rows, key_rows, pair_rows, length)
    probs = jnp.exp(jnp.where(valid, scores, MASKED) - log_totals[..., None])
    low_probs = probs.astype(jnp.bfloat16)
    probs_grad = jnp.einsum(
        "ihe,jhe->hij", mixed_grad, value_rows, preferred_element_type=jnp.float32
    )
    value_grad = jnp.einsum(
        "hij,ihe->jhe", low_probs, mixed_grad, preferred_element_type=jnp.float32
    )
    inner_sum = jnp.sum(probs * probs_grad, -1, keepdims=True)
    score_grad = (probs * (probs_grad - inner_sum) + pair_cot.astype(jnp.float32)).astype(
        jnp.bfloat16
    )
    query_grad = factor * jnp.einsum(
        "hij,jhe->ihe", score_grad, key_rows, preferred_element_type=jnp.float32
    )
    key_grad = factor * jnp.einsum(
        "hij,ihe->jhe", score_grad, query_rows, preferred_element_type=jnp.float32
    )
    return (score_grad, query_grad.astype(jnp.bfloat16), key_grad, value_grad)


def shards(
    atoms,
    pair_bias,
    lengths,
    first_gain,
    first_shift,
    query_weight,
    query_bias,
    key_weight,
    value_weight,
    value_bias,
    out_weight,
    out_bias,
    second_gain,
    second_shift,
    inner_weight,
    inner_bias,
    outer_weight,
    outer_bias,
    atoms_cotangent,
    pair_cotangent,
):
    floats = jnp.float32
    halves = jnp.bfloat16
    molecules, atom_rows, model_width = atoms.shape
    head_count = pair_bias.shape[1]
    head_size = model_width // head_count
    factor = head_size ** (-0.5)
    tokens = molecules * atom_rows
    atoms_float = atoms.astype(floats).reshape(tokens, model_width)
    first_out, first_normed, first_inverse = norm_forward(
        atoms_float, first_gain.astype(floats), first_shift.astype(floats)
    )
    first_low = first_out.astype(halves)
    query_low = (
        jnp.dot(first_low, query_weight, preferred_element_type=floats) + query_bias.astype(floats)
    ).astype(halves)
    first_grouped = first_low.reshape(molecules, atom_rows, model_width)
    key_local, value_local = project_keys(first_grouped, key_weight, value_weight, value_bias)
    all_keys, all_values = (
        lax.all_gather(key_local, "rows", axis=1, tiled=True),
        lax.all_gather(value_local, "rows", axis=1, tiled=True),
    )
    key_count = all_keys.shape[1]
    query_heads = query_low.reshape(molecules, atom_rows, head_count, head_size)
    key_heads = all_keys.reshape(molecules, key_count, head_count, head_size)
    value_heads = all_values.reshape(molecules, key_count, head_count, head_size)
    pair_out, mixed_heads, log_totals = lax.map(
        partial(attend_forward, factor), (query_heads, key_heads, value_heads, pair_bias, lengths)
    )
    mixed_low = mixed_heads.reshape(tokens, model_width)
    middle = (
        atoms_float
        + jnp.dot(mixed_low, out_weight, preferred_element_type=floats)
        + out_bias.astype(floats)
    )
    second_out, second_normed, second_inverse = norm_forward(
        middle, second_gain.astype(floats), second_shift.astype(floats)
    )
    second_low = second_out.astype(halves)
    inner_pre = jnp.dot(
        second_low, inner_weight, preferred_element_type=floats
    ) + inner_bias.astype(floats)
    activated, gelu_pull = jax.vjp(jax.nn.gelu, inner_pre)
    activated_low = activated.astype(halves)
    result_rows = (
        middle
        + jnp.dot(activated_low, outer_weight, preferred_element_type=floats)
        + outer_bias.astype(floats)
    )
    atoms_out = result_rows.astype(halves).reshape(molecules, atom_rows, model_width)
    grad_outer = atoms_cotangent.reshape(tokens, model_width)
    outer_weight_grad = across(activated_low, grad_outer)
    outer_bias_grad = column_sum(grad_outer)
    grad_activated = against(grad_outer, outer_weight)
    grad_inner = gelu_pull(grad_activated)[0].astype(halves)
    inner_weight_grad = across(second_low, grad_inner)
    inner_bias_grad = column_sum(grad_inner)
    grad_second = against(grad_inner, inner_weight)
    second_back, second_gain_grad, second_shift_grad = norm_backward(
        grad_second, second_normed, second_inverse, second_gain.astype(floats)
    )
    grad_middle = grad_outer.astype(floats) + second_back
    grad_branch = grad_middle.astype(halves)
    out_weight_grad = across(mixed_low, grad_branch)
    out_bias_grad = column_sum(grad_branch)
    grad_mixed = against(grad_branch, out_weight).astype(halves)
    pair_grad, query_grad, key_grad, value_grad = lax.map(
        partial(attend_backward, factor),
        (
            query_heads,
            key_heads,
            value_heads,
            pair_bias,
            lengths,
            log_totals,
            grad_mixed.reshape(molecules, atom_rows, head_count, head_size),
            pair_cotangent,
        ),
    )
    key_share, value_share = (
        lax.psum_scatter(
            key_grad.reshape(molecules, key_count, model_width),
            "rows",
            scatter_dimension=1,
            tiled=True,
        ),
        lax.psum_scatter(
            value_grad.reshape(molecules, key_count, model_width),
            "rows",
            scatter_dimension=1,
            tiled=True,
        ),
    )
    key_grad_low = key_share.reshape(tokens, model_width).astype(halves)
    value_grad_low = value_share.reshape(tokens, model_width).astype(halves)
    query_grad_low = query_grad.reshape(tokens, model_width)
    query_weight_grad = across(first_low, query_grad_low)
    query_bias_grad = column_sum(query_grad_low)
    key_weight_grad = across(first_low, key_grad_low)
    value_weight_grad = across(first_low, value_grad_low)
    value_bias_grad = column_sum(value_grad_low)
    grad_first = (
        against(query_grad_low, query_weight)
        + against(key_grad_low, key_weight)
        + against(value_grad_low, value_weight)
    )
    first_back, first_gain_grad, first_shift_grad = norm_backward(
        grad_first, first_normed, first_inverse, first_gain.astype(floats)
    )
    atoms_grad = (
        (grad_middle + first_back).astype(halves).reshape(molecules, atom_rows, model_width)
    )
    (
        first_gain_grad,
        first_shift_grad,
        query_weight_grad,
        query_bias_grad,
        key_weight_grad,
        value_weight_grad,
        value_bias_grad,
        out_weight_grad,
        out_bias_grad,
        second_gain_grad,
        second_shift_grad,
        inner_weight_grad,
        inner_bias_grad,
        outer_weight_grad,
        outer_bias_grad,
    ) = (
        lax.psum_scatter(first_gain_grad, "batch", scatter_dimension=0, tiled=True),
        lax.psum_scatter(first_shift_grad, "batch", scatter_dimension=0, tiled=True),
        lax.psum_scatter(query_weight_grad, "batch", scatter_dimension=0, tiled=True),
        lax.psum_scatter(query_bias_grad, "batch", scatter_dimension=0, tiled=True),
        lax.psum_scatter(key_weight_grad, "batch", scatter_dimension=0, tiled=True),
        lax.psum_scatter(value_weight_grad, "batch", scatter_dimension=0, tiled=True),
        lax.psum_scatter(value_bias_grad, "batch", scatter_dimension=0, tiled=True),
        lax.psum_scatter(out_weight_grad, "batch", scatter_dimension=0, tiled=True),
        lax.psum_scatter(out_bias_grad, "batch", scatter_dimension=0, tiled=True),
        lax.psum_scatter(second_gain_grad, "batch", scatter_dimension=0, tiled=True),
        lax.psum_scatter(second_shift_grad, "batch", scatter_dimension=0, tiled=True),
        lax.psum_scatter(inner_weight_grad, "batch", scatter_dimension=0, tiled=True),
        lax.psum_scatter(inner_bias_grad, "batch", scatter_dimension=0, tiled=True),
        lax.psum_scatter(outer_weight_grad, "batch", scatter_dimension=0, tiled=True),
        lax.psum_scatter(outer_bias_grad, "batch", scatter_dimension=0, tiled=True),
    )
    (
        first_gain_grad,
        first_shift_grad,
        query_weight_grad,
        query_bias_grad,
        key_weight_grad,
        value_weight_grad,
        value_bias_grad,
        out_weight_grad,
        out_bias_grad,
        second_gain_grad,
        second_shift_grad,
        inner_weight_grad,
        inner_bias_grad,
        outer_weight_grad,
        outer_bias_grad,
    ) = (
        lax.psum(first_gain_grad.astype(jnp.bfloat16), "rows").astype(jnp.float32),
        lax.psum(first_shift_grad.astype(jnp.bfloat16), "rows").astype(jnp.float32),
        lax.psum(query_weight_grad.astype(jnp.bfloat16), "rows").astype(jnp.float32),
        lax.psum(query_bias_grad.astype(jnp.bfloat16), "rows").astype(jnp.float32),
        lax.psum(key_weight_grad.astype(jnp.bfloat16), "rows").astype(jnp.float32),
        lax.psum(value_weight_grad.astype(jnp.bfloat16), "rows").astype(jnp.float32),
        lax.psum(value_bias_grad.astype(jnp.bfloat16), "rows").astype(jnp.float32),
        lax.psum(out_weight_grad.astype(jnp.bfloat16), "rows").astype(jnp.float32),
        lax.psum(out_bias_grad.astype(jnp.bfloat16), "rows").astype(jnp.float32),
        lax.psum(second_gain_grad.astype(jnp.bfloat16), "rows").astype(jnp.float32),
        lax.psum(second_shift_grad.astype(jnp.bfloat16), "rows").astype(jnp.float32),
        lax.psum(inner_weight_grad.astype(jnp.bfloat16), "rows").astype(jnp.float32),
        lax.psum(inner_bias_grad.astype(jnp.bfloat16), "rows").astype(jnp.float32),
        lax.psum(outer_weight_grad.astype(jnp.bfloat16), "rows").astype(jnp.float32),
        lax.psum(outer_bias_grad.astype(jnp.bfloat16), "rows").astype(jnp.float32),
    )
    return (
        atoms_out,
        pair_out,
        atoms_grad,
        pair_grad,
        first_gain_grad,
        first_shift_grad,
        query_weight_grad,
        query_bias_grad,
        key_weight_grad,
        value_weight_grad,
        value_bias_grad,
        out_weight_grad,
        out_bias_grad,
        second_gain_grad,
        second_shift_grad,
        inner_weight_grad,
        inner_bias_grad,
        outer_weight_grad,
        outer_bias_grad,
    )


def solution(mesh):
    placed = (
        P("batch", "rows", None),
        P("batch", None, "rows", None),
        P("batch"),
        P(),
        P(),
        P(),
        P(),
        P(),
        P(),
        P(),
        P(),
        P(),
        P(),
        P(),
        P(),
        P(),
        P(),
        P(),
        P("batch", "rows", None),
        P("batch", None, "rows", None),
    )
    return jax.shard_map(
        shards,
        mesh=mesh,
        in_specs=placed,
        out_specs=(
            P("batch", "rows", None),
            P("batch", None, "rows", None),
            P("batch", "rows", None),
            P("batch", None, "rows", None),
            P("batch"),
            P("batch"),
            P("batch", None),
            P("batch"),
            P("batch", None),
            P("batch", None),
            P("batch"),
            P("batch", None),
            P("batch"),
            P("batch"),
            P("batch"),
            P("batch", None),
            P("batch"),
            P("batch", None),
            P("batch"),
        ),
        check_vma=False,
    )
```

profile of v0, /device:TPU:0, one launch (start us, length us, event | category | flops | bytes accessed | tf_op | source)
XLA Modules:
  0.0 693.5 jit_solution(6744688574644620447)
XLA Ops:
  12.9 2.1 fusion.125
  21.6 3.7 fusion.144
  25.2 20.6 %all-gather.5.cloned.1.call-done = bf16[4,256,512]{2,1,0:T(8,128)(2,1)} async-done(((bf16[4,64,512]{2,1,0:T(8,128)(2,1)}), bf16[4,256,512]{2,1,0:T(8,128)(2,1)}) %all-gather.5.cloned.1.call-update) | async-done | bytes 1048592 | tf_op jit(solution)/shard_map/all_gather | solution.py:147
  45.9 2.3 copy.61
  48.2 27.3 %all-gather.3.cloned.1.call-done = bf16[4,256,512]{2,1,0:T(8,128)(2,1)} async-done(((bf16[4,64,512]{2,1,0:T(8,128)(2,1)}), bf16[4,256,512]{2,1,0:T(8,128)(2,1)}) %all-gather.3.cloned.1.call-update) | async-done | bytes 1048592 | tf_op jit(solution)/shard_map/all_gather | solution.py:146
  77.8 4.5 broadcast.188.clone
  82.3 43.1 %while.30 = (s32[]{:T(128)}, bf16[4,64,64,256]{3,2,1,0:T(8,128)(2,1)}, bf16[4,64,64,8]{1,3,2,0:T(8,128)(2,1)}, f32[4,64,64]{2,1,0:T(8,128)S(1)}, bf16[4,64,64,8]...) while((s32[]{:T(128)}, ...), condition=%wide.region_5.6_spmd, body=%wide.region_2.5_spmd.sunk | while | flops 47214848 | bytes 21941888 | solution.py:153
  84.2 3.8 bitcast_dynamic-update-slice_fusion.6
  90.0 3.0 fusion.206
  95.0 3.8 bitcast_dynamic-update-slice_fusion.6
  100.8 3.0 fusion.206
  105.8 3.8 bitcast_dynamic-update-slice_fusion.6
  111.6 3.0 fusion.206
  116.5 3.8 bitcast_dynamic-update-slice_fusion.6
  122.4 3.0 fusion.206
  125.4 2.5 copy.63
  128.0 2.2 reshape.262
  130.1 1.7 fusion.143
  132.1 4.8 convert_reduce_fusion
  141.0 4.5 broadcast.188
  145.5 124.5 %while.31 = (s32[]{:T(128)}, bf16[4,64,64,256]{3,2,1,0:T(8,128)(2,1)}, bf16[4,64,64,8]{1,3,2,0:T(8,128)(2,1)}, f32[4,256,64,8]{1,3,2,0:T(8,128)}, f32[4,256,64,8...) while((s32[]{:T(128)}, ...), condition=%wide.region_12.13_spmd, body=%wide.region_10.12_spmd.sunk | while | flops 193147904 | bytes 48575392 | solution.py:193
  147.4 5.2 fusion.229
  152.5 6.8 fusion.230
  159.3 3.4 fusion.232
  162.7 7.0 %fusion.231 = f32[4,256,64,8]{1,3,2,0:T(8,128)} fusion(f32[4,256,64,8]{1,3,2,0:T(8,128)} %get-tuple-element.487, s32[]{:T(128)S(6)} %copy.94, f32[64,64,256]{2,1,0:T(8,128)} %fusion.229, bf16[4,64,64,256]{3,2,1,0:T(8,128)(2,1)} %get-tuple-element.510, bf16[4,256,64,8]{1,3,2,0:T(8,128)(2,1)S(1)} %get-tuple-element.509, ...), kind=kOutput, calls=%fused_computation.37.clone.1 | convolution fusion | flops 56758528 | bytes 11931136 | tf_op jit(solution)/shard_map/while/body/eval_jaxpr/hij,ihe->jhe/dot_general | solution.py:100
  169.6 6.9 %bitcast_dynamic-update-slice_fusion.8 = bf16[4,64,64,256]{3,2,1,0:T(8,128)(2,1)} fusion(bf16[4,64,64,256]{3,2,1,0:T(8,128)(2,1)} %get-tuple-element.485, s32[]{:T(128)S(6)} %copy.94, bf16[4,64,64,256]{3,2,1,0:T(8,128)(2,1)} %get-tuple-element.510, f32[64,64,256]{2,1,0:T(8,128)} %fusion.229, bf16[4,256,64,8]{1,3,2,0:T(8,128)(2,1)S(1)} %get-tuple-element.509, ...), kind=kOutput, calls=%fused_computation.30.clone.1 | convolution fusion | flops 39850240 | bytes 13371904 | tf_op jit(solution)/shard_map/while/body/eval_jaxpr/sub | solution.py:94
  178.5 5.1 fusion.229
  183.6 6.8 fusion.230
  190.4 3.4 fusion.232
  193.8 7.0 %fusion.231 = f32[4,256,64,8]{1,3,2,0:T(8,128)} fusion(f32[4,256,64,8]{1,3,2,0:T(8,128)} %get-tuple-element.487, s32[]{:T(128)S(6)} %copy.94, f32[64,64,256]{2,1,0:T(8,128)} %fusion.229, bf16[4,64,64,256]{3,2,1,0:T(8,128)(2,1)} %get-tuple-element.510, bf16[4,256,64,8]{1,3,2,0:T(8,128)(2,1)S(1)} %get-tuple-element.509, ...), kind=kOutput, calls=%fused_computation.37.clone.1 | convolution fusion | flops 56758528 | bytes 11931136 | tf_op jit(solution)/shard_map/while/body/eval_jaxpr/hij,ihe->jhe/dot_general | solution.py:100
  200.8 6.9 %bitcast_dynamic-update-slice_fusion.8 = bf16[4,64,64,256]{3,2,1,0:T(8,128)(2,1)} fusion(bf16[4,64,64,256]{3,2,1,0:T(8,128)(2,1)} %get-tuple-element.485, s32[]{:T(128)S(6)} %copy.94, bf16[4,64,64,256]{3,2,1,0:T(8,128)(2,1)} %get-tuple-element.510, f32[64,64,256]{2,1,0:T(8,128)} %fusion.229, bf16[4,256,64,8]{1,3,2,0:T(8,128)(2,1)S(1)} %get-tuple-element.509, ...), kind=kOutput, calls=%fused_computation.30.clone.1 | convolution fusion | flops 39850240 | bytes 13371904 | tf_op jit(solution)/shard_map/while/body/eval_jaxpr/sub | solution.py:94
  209.6 5.2 fusion.229
  214.8 6.8 fusion.230
  221.6 3.4 fusion.232
  224.9 7.0 %fusion.231 = f32[4,256,64,8]{1,3,2,0:T(8,128)} fusion(f32[4,256,64,8]{1,3,2,0:T(8,128)} %get-tuple-element.487, s32[]{:T(128)S(6)} %copy.94, f32[64,64,256]{2,1,0:T(8,128)} %fusion.229, bf16[4,64,64,256]{3,2,1,0:T(8,128)(2,1)} %get-tuple-element.510, bf16[4,256,64,8]{1,3,2,0:T(8,128)(2,1)S(1)} %get-tuple-element.509, ...), kind=kOutput, calls=%fused_computation.37.clone.1 | convolution fusion | flops 56758528 | bytes 11931136 | tf_op jit(solution)/shard_map/while/body/eval_jaxpr/hij,ihe->jhe/dot_general | solution.py:100
  231.9 6.9 %bitcast_dynamic-update-slice_fusion.8 = bf16[4,64,64,256]{3,2,1,0:T(8,128)(2,1)} fusion(bf16[4,64,64,256]{3,2,1,0:T(8,128)(2,1)} %get-tuple-element.485, s32[]{:T(128)S(6)} %copy.94, bf16[4,64,64,256]{3,2,1,0:T(8,128)(2,1)} %get-tuple-element.510, f32[64,64,256]{2,1,0:T(8,128)} %fusion.229, bf16[4,256,64,8]{1,3,2,0:T(8,128)(2,1)S(1)} %get-tuple-element.509, ...), kind=kOutput, calls=%fused_computation.30.clone.1 | convolution fusion | flops 39850240 | bytes 13371904 | tf_op jit(solution)/shard_map/while/body/eval_jaxpr/sub | solution.py:94
  240.7 5.2 fusion.229
  245.9 6.8 fusion.230
  252.7 3.4 fusion.232
  256.1 7.0 %fusion.231 = f32[4,256,64,8]{1,3,2,0:T(8,128)} fusion(f32[4,256,64,8]{1,3,2,0:T(8,128)} %get-tuple-element.487, s32[]{:T(128)S(6)} %copy.94, f32[64,64,256]{2,1,0:T(8,128)} %fusion.229, bf16[4,64,64,256]{3,2,1,0:T(8,128)(2,1)} %get-tuple-element.510, bf16[4,256,64,8]{1,3,2,0:T(8,128)(2,1)S(1)} %get-tuple-element.509, ...), kind=kOutput, calls=%fused_computation.37.clone.1 | convolution fusion | flops 56758528 | bytes 11931136 | tf_op jit(solution)/shard_map/while/body/eval_jaxpr/hij,ihe->jhe/dot_general | solution.py:100
  263.0 6.9 %bitcast_dynamic-update-slice_fusion.8 = bf16[4,64,64,256]{3,2,1,0:T(8,128)(2,1)} fusion(bf16[4,64,64,256]{3,2,1,0:T(8,128)(2,1)} %get-tuple-element.485, s32[]{:T(128)S(6)} %copy.94, bf16[4,64,64,256]{3,2,1,0:T(8,128)(2,1)} %get-tuple-element.510, f32[64,64,256]{2,1,0:T(8,128)} %fusion.229, bf16[4,256,64,8]{1,3,2,0:T(8,128)(2,1)S(1)} %get-tuple-element.509, ...), kind=kOutput, calls=%fused_computation.30.clone.1 | convolution fusion | flops 39850240 | bytes 13371904 | tf_op jit(solution)/shard_map/while/body/eval_jaxpr/sub | solution.py:94
  270.0 2.9 copy.69
  273.0 2.9 copy.68
  280.7 35.7 %reduce-scatter.11.cloned.1.call-done = f32[4,64,512]{2,1,0:T(8,128)} async-done(((f32[4,256,512]{2,1,0:T(8,128)}), f32[4,64,512]{2,1,0:T(8,128)}) %reduce-scatter.11.cloned.1.call-update) | async-done | bytes 524304 | tf_op jit(solution)/shard_map/reduce_scatter | solution.py:213
  319.0 43.0 %reduce-scatter.9.cloned.1.call-done = f32[4,64,512]{2,1,0:T(8,128)} async-done(((f32[4,256,512]{2,1,0:T(8,128)}), f32[4,64,512]{2,1,0:T(8,128)}) %reduce-scatter.9.cloned.1.call-update) | async-done | bytes 524304 | tf_op jit(solution)/shard_map/reduce_scatter | solution.py:207
  365.1 2.9 fusion.133
  369.4 2.8 fusion.132
  375.5 3.9 fusion.123
  379.3 20.9 %reduce-scatter.19.cloned.1.call-done = f32[64,512]{1,0:T(8,128)} async-done(((f32[512,512]{1,0:T(8,128)}), f32[64,512]{1,0:T(8,128)}) %reduce-scatter.19.cloned.1.call-update) | async-done | bytes 131088 | tf_op jit(solution)/shard_map/reduce_scatter | solution.py:263
  401.8 37.5 %reduce-scatter.13.cloned.1.call-done = f32[64,512]{1,0:T(8,128)} async-done(((f32[512,512]{1,0:T(8,128)}), f32[64,512]{1,0:T(8,128)}) %reduce-scatter.13.cloned.1.call-update) | async-done | bytes 131088 | tf_op jit(solution)/shard_map/reduce_scatter | solution.py:258
  439.4 1.5 convert_element_type.273
  442.1 36.5 %reduce-scatter.17.cloned.1.call-done = f32[64,512]{1,0:T(8,128)} async-done(((f32[512,512]{1,0:T(8,128)}), f32[64,512]{1,0:T(8,128)}) %reduce-scatter.17.cloned.1.call-update) | async-done | bytes 131088 | tf_op jit(solution)/shard_map/reduce_scatter | solution.py:261
  480.1 37.7 %reduce-scatter.15.cloned.1.call-done = f32[64,512]{1,0:T(8,128)} async-done(((f32[512,512]{1,0:T(8,128)}), f32[64,512]{1,0:T(8,128)}) %reduce-scatter.15.cloned.1.call-update) | async-done | bytes 131088 | tf_op jit(solution)/shard_map/reduce_scatter | solution.py:260
  519.3 53.2 %reduce-scatter.23.cloned.1.call-done = f32[256,512]{1,0:T(8,128)} async-done(((f32[2048,512]{1,0:T(8,128)}), f32[256,512]{1,0:T(8,128)}) %reduce-scatter.23.cloned.1.call-update) | async-done | bytes 524304 | tf_op jit(solution)/shard_map/reduce_scatter | solution.py:269
  572.5 1.8 convert_element_type.299
  574.3 53.1 %reduce-scatter.21.cloned.1.call-done = f32[64,2048]{1,0:T(8,128)} async-done(((f32[512,2048]{1,0:T(8,128)}), f32[64,2048]{1,0:T(8,128)}) %reduce-scatter.21.cloned.1.call-update) | async-done | bytes 524304 | tf_op jit(solution)/shard_map/reduce_scatter | solution.py:267
  627.4 1.8 convert_element_type.294
  629.2 2.6 multiply_reduce_fusion.2
  631.8 24.1 %all-reduce.9 = (bf16[512]{0:T(512)(128)(2,1)S(1)}, bf16[512]{0:T(512)(128)(2,1)S(1)}, bf16[512]{0:T(512)(128)(2,1)S(1)}, bf16[512]{0:T(512)(128)(2,1)S(1)}, bf1...) all-reduce(f32[512]{0:T(512)S(1)} %get-tuple-element.213, ...), channel_id=4, replica_groups=mesh['batch'=8,'rows'=4] {'batch'}, use_global_device_ids=true, to_apply=%region_18.19.clone | all-reduce | flops 6144 | bytes 36864
  656.6 12.1 %all-reduce.10 = (bf16[64]{0:T(256)(128)(2,1)S(1)}, bf16[64]{0:T(256)(128)(2,1)S(1)}, bf16[64]{0:T(256)(128)(2,1)S(1)}, bf16[64]{0:T(256)(128)(2,1)S(1)}, bf16[6...) all-reduce(bf16[64]{0:T(256)(128)(2,1)S(1)} %dynamic-slice.35, ...), channel_id=1, replica_groups=mesh['batch'=8,'rows'=4] {'rows'}, use_global_device_ids=true, to_apply=%region_19.20 | all-reduce | flops 768 | bytes 3072 | tf_op jit(solution)/shard_map/psum | solution.py:289
  673.4 2.0 add_convert_fusion
  675.4 2.1 all-reduce.14.cloned.1.call-done
  683.4 1.8 convert_element_type.295
  685.2 1.8 convert_element_type.300
  (225 shorter events, 72.8 us)
Async XLA Ops:
  7.2 124.8 %copy-start = (bf16[512,2048]{1,0:T(8,128)(2,1)S(1)}, bf16[512,2048]{1,0:T(8,128)(2,1)}, u32[]{:S(2)}) copy-start(bf16[512,2048]{1,0:T(8,128)(2,1)} %param.38) | copy-start | bytes 6291460
  7.2 9.9 %copy-start.5 = (bf16[4,64,512]{2,1,0:T(8,128)(2,1)S(1)}, bf16[4,64,512]{2,1,0:T(8,128)(2,1)}, u32[]{:S(2)}) copy-start(bf16[4,64,512]{2,1,0:T(8,128)(2,1)} %param.24) | copy-start | bytes 786436
  7.2 7.9 %copy-start.20 = (bf16[512,512]{1,0:T(8,128)(2,1)S(1)}, bf16[512,512]{1,0:T(8,128)(2,1)}, u32[]{:S(2)}) copy-start(bf16[512,512]{1,0:T(8,128)(2,1)} %param.31) | copy-start | bytes 1572868
  7.2 9.2 %copy-start.40 = (bf16[512]{0:T(512)(128)(2,1)S(1)}, bf16[512]{0:T(512)(128)(2,1)}, u32[]{:S(2)}) copy-start(bf16[512]{0:T(512)(128)(2,1)} %param.36) | copy-start | bytes 3076
  7.2 9.2 %copy-start.41 = (bf16[512]{0:T(512)(128)(2,1)S(1)}, bf16[512]{0:T(512)(128)(2,1)}, u32[]{:S(2)}) copy-start(bf16[512]{0:T(512)(128)(2,1)} %param.37) | copy-start | bytes 3076
  7.3 9.2 %copy-start.42 = (bf16[512]{0:T(512)(128)(2,1)S(1)}, bf16[512]{0:T(512)(128)(2,1)}, u32[]{:S(2)}) copy-start(bf16[512]{0:T(512)(128)(2,1)} %param.30) | copy-start | bytes 3076
  7.3 9.2 %copy-start.43 = (bf16[512]{0:T(512)(128)(2,1)S(1)}, bf16[512]{0:T(512)(128)(2,1)}, u32[]{:S(2)}) copy-start(bf16[512]{0:T(512)(128)(2,1)} %param.35) | copy-start | bytes 3076
  7.3 9.2 %copy-start.37 = (bf16[2048]{0:T(1024)(128)(2,1)S(1)}, bf16[2048]{0:T(1024)(128)(2,1)}, u32[]{:S(2)}) copy-start(bf16[2048]{0:T(1024)(128)(2,1)} %param.39) | copy-start | bytes 12292
  7.3 38.6 %all-gather.5.cloned.1.call-start = ((), (), s32[]{:S(2)}) async-start(), calls=%async_computation.9 | async-start | bytes 1310720 | tf_op jit(solution)/shard_map/all_gather | solution.py:147
  12.9 5.7 copy-start.6
  15.1 60.4 %all-gather.3.cloned.1.call-start = ((), (), s32[]{:S(2)}) async-start(), calls=%async_computation.8 | async-start | bytes 1310720 | tf_op jit(solution)/shard_map/all_gather | solution.py:146
  16.2 5.4 copy-start.12
  16.2 300.3 %reduce-scatter.11.cloned.1.call-start = ((), (), s32[]{:S(2)}) async-start(), calls=%async_computation.11 | async-start | bytes 2621440 | tf_op jit(solution)/shard_map/reduce_scatter | solution.py:213
  16.3 0.8 copy-start.31
  16.4 0.7 copy-start.33
  130.1 1.9 copy-start.22
  131.8 6.5 copy-start.3
  132.1 6.2 copy-start.29
  136.8 1.4 copy-start.25
  136.8 1.4 copy-start.13
  138.3 1.0 copy-start.23
  139.1 136.9 %copy-start.8 = (f32[256,512]{1,0:T(8,128)}, f32[256,512]{1,0:T(8,128)S(1)}, u32[]{:S(2)}) copy-start(f32[256,512]{1,0:T(8,128)S(1)} %get-tuple-element.290) | copy-start | bytes 1572868
  141.0 4.5 copy-start.2
  272.9 89.0 %reduce-scatter.9.cloned.1.call-start = ((), (), s32[]{:S(2)}) async-start(), calls=%async_computation.10 | async-start | bytes 2621440 | tf_op jit(solution)/shard_map/reduce_scatter | solution.py:207
  275.9 0.9 copy-start.15
  275.9 2.3 copy-start.11
  275.9 3.3 copy-start.7
  275.9 124.3 %reduce-scatter.19.cloned.1.call-start = ((), (), s32[]{:S(2)}) async-start(), calls=%async_computation.15 | async-start | bytes 1179648 | tf_op jit(solution)/shard_map/reduce_scatter | solution.py:263
  278.2 161.2 %reduce-scatter.13.cloned.1.call-start = ((), (), s32[]{:S(2)}) async-start(), calls=%async_computation.12 | async-start | bytes 1179648 | tf_op jit(solution)/shard_map/reduce_scatter | solution.py:258
  279.2 39.6 %copy-start.16 = (bf16[256,512]{0,1:T(8,128)(2,1)}, bf16[256,512]{0,1:T(8,128)(2,1)S(1)}, u32[]{:S(2)}) copy-start(bf16[256,512]{0,1:T(8,128)(2,1)S(1)} %reshape.266) | copy-start | bytes 786436
  280.7 197.9 %reduce-scatter.17.cloned.1.call-start = ((), (), s32[]{:S(2)}) async-start(), calls=%async_computation.14 | async-start | bytes 1179648 | tf_op jit(solution)/shard_map/reduce_scatter | solution.py:261
  317.6 1.3 copy-start.27
  318.9 46.2 %copy-start.10 = (f32[256,2048]{1,0:T(8,128)S(1)}, f32[256,2048]{1,0:T(8,128)}, u32[]{:S(2)}) copy-start(f32[256,2048]{1,0:T(8,128)} %get-tuple-element.297) | copy-start | bytes 6291460
  318.9 46.2 %copy-start.14 = (bf16[4,64,512]{2,1,0:T(8,128)(2,1)S(1)}, bf16[4,64,512]{2,1,0:T(8,128)(2,1)}, u32[]{:S(2)}) copy-start(bf16[4,64,512]{2,1,0:T(8,128)(2,1)} %param.42) | copy-start | bytes 786436
  318.9 198.9 %reduce-scatter.15.cloned.1.call-start = ((), (), s32[]{:S(2)}) async-start(), calls=%async_computation.13 | async-start | bytes 1179648 | tf_op jit(solution)/shard_map/reduce_scatter | solution.py:260
  363.0 0.7 copy-start.18
  365.0 207.5 %reduce-scatter.23.cloned.1.call-start = ((), (), s32[]{:S(2)}) async-start(), calls=%async_computation.17 | async-start | bytes 4718592 | tf_op jit(solution)/shard_map/reduce_scatter | solution.py:269
  368.0 1.0 copy-start.4
  368.0 1.4 copy-start.26
  368.0 1.4 copy-start.30
  368.0 259.4 %reduce-scatter.21.cloned.1.call-start = ((), (), s32[]{:S(2)}) async-start(), calls=%async_computation.16 | async-start | bytes 4718592 | tf_op jit(solution)/shard_map/reduce_scatter | solution.py:267
  372.2 0.7 copy-start.45
  372.2 2.5 copy-start.44
  372.2 2.9 copy-start.17
  372.2 2.9 copy-start.24
  372.2 305.2 %all-reduce.14.cloned.1.call-start = ((), (), s32[]{:S(2)}) async-start(), calls=%async_computation.18 | async-start | bytes 1572864 | tf_op jit(solution)/shard_map/psum | solution.py:291
  375.5 65.5 %copy-start.19 = (bf16[4,64,512]{2,1,0:T(8,128)(2,1)S(1)}, bf16[4,64,512]{2,1,0:T(8,128)(2,1)}, u32[]{:S(2)}) copy-start(bf16[4,64,512]{2,1,0:T(8,128)(2,1)} %copy-done.18) | copy-start | bytes 786436
  375.5 65.4 %copy-start.21 = (bf16[512,512]{1,0:T(8,128)(2,1)S(1)}, bf16[512,512]{1,0:T(8,128)(2,1)}, u32[]{:S(2)}) copy-start(bf16[512,512]{1,0:T(8,128)(2,1)} %param.31) | copy-start | bytes 1572868
  440.9 188.3 %copy-start.28 = (bf16[4,64,512]{2,1,0:T(8,128)(2,1)S(1)}, bf16[4,64,512]{2,1,0:T(8,128)(2,1)}, u32[]{:S(2)}) copy-start(bf16[4,64,512]{2,1,0:T(8,128)(2,1)} %copy-done.27) | copy-start | bytes 786436
  440.9 188.3 %copy-start.32 = (f32[256]{0:T(256)S(1)}, f32[256]{0:T(256)}, u32[]{:S(2)}) copy-start(f32[256]{0:T(256)} %copy-done.31) | copy-start | bytes 3076
  440.9 188.3 %copy-start.34 = (f32[256]{0:T(256)S(1)}, f32[256]{0:T(256)}, u32[]{:S(2)}) copy-start(f32[256]{0:T(256)} %copy-done.33) | copy-start | bytes 3076
  574.3 57.5 %copy-start.35 = (f32[512]{0:T(512)S(1)}, f32[512]{0:T(512)}, u32[]{:S(2)}) copy-start(f32[512]{0:T(512)} %get-tuple-element.289) | copy-start | bytes 6148
  574.3 57.5 %copy-start.36 = (f32[2048]{0:T(1024)S(1)}, f32[2048]{0:T(1024)}, u32[]{:S(2)}) copy-start(f32[2048]{0:T(1024)} %get-tuple-element.287) | copy-start | bytes 24580
  574.3 57.5 %copy-start.38 = (f32[512]{0:T(512)S(1)}, f32[512]{0:T(512)}, u32[]{:S(2)}) copy-start(f32[512]{0:T(512)} %get-tuple-element.211) | copy-start | bytes 6148
  574.3 57.5 %copy-start.39 = (f32[512]{0:T(512)S(1)}, f32[512]{0:T(512)}, u32[]{:S(2)}) copy-start(f32[512]{0:T(512)} %get-tuple-element.217) | copy-start | bytes 6148
  574.3 99.1 %copy-start.9 = (f32[256,512]{1,0:T(8,128)S(1)}, f32[256,512]{1,0:T(8,128)}, u32[]{:S(2)}) copy-start(f32[256,512]{1,0:T(8,128)} %copy-done.8) | copy-start | bytes 1572868
  629.2 57.8 %copy-start.1 = (bf16[512,2048]{1,0:T(8,128)(2,1)S(1)}, bf16[512,2048]{1,0:T(8,128)(2,1)}, u32[]{:S(2)}) copy-start(bf16[512,2048]{1,0:T(8,128)(2,1)} %param.38) | copy-start | bytes 6291460
Sparse Core Ops, SparseCore 0:
  15.2 30.6 all-gather.4
  48.0 27.4 all-gather.2
  273.1 43.3 reduce-scatter.10
  318.7 43.1 reduce-scatter.8
  364.9 35.3 reduce-scatter.18
  403.3 35.9 reduce-scatter.12
  442.5 35.9 reduce-scatter.16
  481.7 35.9 reduce-scatter.14
  521.1 51.3 reduce-scatter.22
  576.1 51.2 reduce-scatter.20
  631.4 45.9 all-reduce.13
where the time goes:
time: 696 us; the launch traced here: 694 us
  waiting for transfers between devices  368 us (53%)
  matrix products  179 us (26%)
  other arithmetic  49.1 us (7%)
  local copies, waits for them, and re-layouts  44.4 us (6%)
  blocking collectives  36.2 us (5%)
  between operations  15.8 us (2%)
    reduce_scatter x1, waiting for transfers between devices, shards(): lax.psum_scatter(outer_weight_grad, 'batch', scatter_dimension=0, tiled=T...  53.2 us
    reduce_scatter x1, waiting for transfers between devices, shards(): lax.psum_scatter(inner_weight_grad, 'batch', scatter_dimension=0, tiled=T...  53.1 us
    reduce_scatter x1, waiting for transfers between devices, shards(): lax.psum_scatter(key_grad.reshape(molecules, key_count, model_width), 'ro...  43 us
    reduce_scatter x1, waiting for transfers between devices, shards(): lax.psum_scatter(key_weight_grad, 'batch', scatter_dimension=0, tiled=True)  37.7 us
    reduce_scatter x1, waiting for transfers between devices, shards(): lax.psum_scatter(query_weight_grad, 'batch', scatter_dimension=0, tiled=T...  37.5 us
    reduce_scatter x1, waiting for transfers between devices, shards(): lax.psum_scatter(value_weight_grad, 'batch', scatter_dimension=0, tiled=T...  36.5 us
    dot_general x8, matrix products, scores_of(): jnp.einsum('ihe,jhe->hij', query_rows, key_rows, preferred_element_type=j...  35.8 us
    reduce_scatter x1, waiting for transfers between devices, shards(): lax.psum_scatter(value_grad.reshape(molecules, key_count, model_width), '...  35.7 us
  transfers between devices with their start and end apart: 11, of which 11 were waited for; matrix products, arithmetic and copies ran while one was open for 8% of the time, Pallas kernels for 0%

commit v1 on v0

--- a/solution.py
+++ b/solution.py
@@ -6,6 +6,19 @@
 
 EPSILON = 1e-05
 MASKED = -1000000000.0
+
+
+def gather_around(shard, axis, dim):
+    ways = lax.axis_size(axis)
+    up = [(d, (d + 1) % ways) for d in range(ways)]
+    down = [(d, (d - 1) % ways) for d in range(ways)]
+    earlier, later = ([shard], [shard])
+    for _ in range(ways // 2):
+        earlier.append(lax.ppermute(earlier[-1], axis, up))
+    for _ in range((ways - 1) // 2):
+        later.append(lax.ppermute(later[-1], axis, down))
+    line = jnp.concatenate([*earlier[::-1], *later[1:]], axis=dim)
+    return jnp.roll(line, (lax.axis_index(axis) - ways // 2) * shard.shape[dim], axis=dim)
 
 
 def norm_forward(values_in, gain, shift):
@@ -144,7 +157,7 @@
     key_local, value_local = project_keys(first_grouped, key_weight, value_weight, value_bias)
     all_keys, all_values = (
         lax.all_gather(key_local, "rows", axis=1, tiled=True),
-        lax.all_gather(value_local, "rows", axis=1, tiled=True),
+        gather_around(value_local, "rows", 1),
     )
     key_count = all_keys.shape[1]
     query_heads = query_low.reshape(molecules, atom_rows, head_count, head_size)

time: 696 us -> 678 us (0.974)
  waiting for transfers between devices: 368 us -> 337 us
  starting transfers between devices: 0.68 us -> 8.29 us
    all_gather x1, waiting for transfers between devices: 27.3 us -> 2.6 us  [shards(): lax.all_gather(key_local, 'rows', axis=1, tiled=True)]
    all_gather x1 -> x0, waiting for transfers between devices: 20.6 us -> none  [shards(): lax.all_gather(value_local, 'rows', axis=1, tiled=True)]
    ppermute x0 -> x3, waiting for transfers between devices: none -> 13.2 us  [the longest x2 13.2 us: gather_around(): earlier.append(lax.ppermute(earlier[-1], axis, up))]
    ppermute x0 -> x3, starting transfers between devices: none -> 7.66 us  [the longest x1 5.1 us: gather_around(): later.append(lax.ppermute(later[-1], axis, down))]
  transfers between devices with their start and end apart: 11 -> 13, of which waited for: 11 -> 12; matrix products, arithmetic and copies ran while one was open for 8% -> 9% of each run, Pallas kernels for 0% -> 0%
where the time goes in v1:
time: 678 us; the launch traced here: 676 us
  waiting for transfers between devices  337 us (50%)
  matrix products  179 us (26%)
  other arithmetic  51.2 us (8%)
  local copies, waits for them, and re-layouts  47.8 us (7%)
  blocking collectives  36.2 us (5%)
  between operations  16.1 us (2%)
  starting transfers between devices  8.29 us (1%)
    reduce_scatter x1, waiting for transfers between devices, shards(): lax.psum_scatter(inner_weight_grad, 'batch', scatter_dimension=0, tiled=T...  53.3 us
    reduce_scatter x1, waiting for transfers between devices, shards(): lax.psum_scatter(outer_weight_grad, 'batch', scatter_dimension=0, tiled=T...  53.1 us
    reduce_scatter x1, waiting for transfers between devices, shards(): lax.psum_scatter(key_grad.reshape(molecules, key_count, model_width), 'ro...  43.2 us
    reduce_scatter x1, waiting for transfers between devices, shards(): lax.psum_scatter(key_weight_grad, 'batch', scatter_dimension=0, tiled=True)  37.7 us
    reduce_scatter x1, waiting for transfers between devices, shards(): lax.psum_scatter(query_weight_grad, 'batch', scatter_dimension=0, tiled=T...  37.5 us
    reduce_scatter x1, waiting for transfers between devices, shards(): lax.psum_scatter(value_grad.reshape(molecules, key_count, model_width), '...  37.3 us
    reduce_scatter x1, waiting for transfers between devices, shards(): lax.psum_scatter(value_weight_grad, 'batch', scatter_dimension=0, tiled=T...  36.4 us
    dot_general x8, matrix products, scores_of(): jnp.einsum('ihe,jhe->hij', query_rows, key_rows, preferred_element_type=j...  35.8 us
  transfers between devices with their start and end apart: 13, of which 12 were waited for; matrix products, arithmetic and copies ran while one was open for 9% of the time, Pallas kernels for 0%

profile of v1, /device:TPU:0, one launch (start us, length us, event | category | flops | bytes accessed | tf_op | source)
XLA Modules:
  0.0 675.8 jit_solution(6675213570879709359)
XLA Ops:
  14.4 5.1 collective-permute-start.2
  28.3 3.4 collective-permute-done
  31.7 2.6 collective-permute-start.1
  34.2 3.7 fusion.144
  37.9 9.8 %collective-permute-done.1 = bf16[4,64,512]{2,1,0:T(8,128)(2,1)S(1)} collective-permute-done((bf16[4,64,512]{2,1,0:T(8,128)(2,1)}, bf16[4,64,512]{2,1,0:T(8,128)(2,1)S(1)}, u32[]{:S(2)}, u32[]{:S(2)}) %collective-permute-start.1) | collective-permute-done | bytes 262176 | tf_op jit(solution)/shard_map/ppermute | solution.py:17
  53.1 2.6 all-gather.2.cloned.1.call-done
  58.0 4.5 broadcast.189.clone
  62.5 43.1 %while.30 = (s32[]{:T(128)}, bf16[4,64,64,256]{3,2,1,0:T(8,128)(2,1)}, bf16[4,64,64,8]{1,3,2,0:T(8,128)(2,1)}, f32[4,64,64]{2,1,0:T(8,128)S(1)}, bf16[4,64,64,8]...) while((s32[]{:T(128)}, ...), condition=%wide.region_5.6_spmd, body=%wide.region_2.5_spmd.sunk | while | flops 47214848 | bytes 21941888 | solution.py:166
  64.4 3.8 bitcast_dynamic-update-slice_fusion.6
  70.2 3.0 fusion.206
  75.2 3.8 bitcast_dynamic-update-slice_fusion.6
  81.0 3.0 fusion.206
  86.0 3.8 bitcast_dynamic-update-slice_fusion.6
  91.8 3.0 fusion.206
  96.8 3.8 bitcast_dynamic-update-slice_fusion.6
  102.6 3.0 fusion.206
  105.7 2.5 copy.61
  108.2 2.2 reshape.262
  110.4 1.7 fusion.143
  112.3 4.8 convert_reduce_fusion
  121.2 4.5 broadcast.189
  125.7 124.5 %while.31 = (s32[]{:T(128)}, bf16[4,64,64,256]{3,2,1,0:T(8,128)(2,1)}, bf16[4,64,64,8]{1,3,2,0:T(8,128)(2,1)}, f32[4,256,64,8]{1,3,2,0:T(8,128)}, f32[4,256,64,8...) while((s32[]{:T(128)}, ...), condition=%wide.region_12.13_spmd, body=%wide.region_10.12_spmd.sunk | while | flops 193147904 | bytes 48575392 | solution.py:206
  127.6 5.1 fusion.229
  132.8 6.8 %fusion.230 = bf16[4,64,64,8]{1,3,2,0:T(8,128)(2,1)} fusion(bf16[4,64,64,8]{1,3,2,0:T(8,128)(2,1)} %get-tuple-element.486, s32[]{:T(128)S(6)} %copy.99, bf16[4,256,64,8]{1,3,2,0:T(8,128)(2,1)S(1)} %get-tuple-element.505, f32[64,64,256]{2,1,0:T(8,128)} %fusion.229, bf16[4,64,64,256]{3,2,1,0:T(8,128)(2,1)} %get-tuple-element.510, ...), kind=kOutput, calls=%fused_computation.41.clone.1 | convolution fusion | flops 56692992 | bytes 11668992 | tf_op jit(solution)/shard_map/while/body/eval_jaxpr/hij,jhe->ihe/dot_general | solution.py:110
  139.5 3.4 fusion.232
  142.9 7.0 %fusion.231 = f32[4,256,64,8]{1,3,2,0:T(8,128)} fusion(f32[4,256,64,8]{1,3,2,0:T(8,128)} %get-tuple-element.487, s32[]{:T(128)S(6)} %copy.99, f32[64,64,256]{2,1,0:T(8,128)} %fusion.229, bf16[4,64,64,256]{3,2,1,0:T(8,128)(2,1)} %get-tuple-element.510, bf16[4,256,64,8]{1,3,2,0:T(8,128)(2,1)S(1)} %get-tuple-element.509, ...), kind=kOutput, calls=%fused_computation.37.clone.1 | convolution fusion | flops 56758528 | bytes 11931136 | tf_op jit(solution)/shard_map/while/body/eval_jaxpr/hij,ihe->jhe/dot_general | solution.py:113
  149.9 6.9 %bitcast_dynamic-update-slice_fusion.8 = bf16[4,64,64,256]{3,2,1,0:T(8,128)(2,1)} fusion(bf16[4,64,64,256]{3,2,1,0:T(8,128)(2,1)} %get-tuple-element.485, s32[]{:T(128)S(6)} %copy.99, bf16[4,64,64,256]{3,2,1,0:T(8,128)(2,1)} %get-tuple-element.510, f32[64,64,256]{2,1,0:T(8,128)} %fusion.229, bf16[4,256,64,8]{1,3,2,0:T(8,128)(2,1)S(1)} %get-tuple-element.509, ...), kind=kOutput, calls=%fused_computation.30.clone.1 | convolution fusion | flops 39850240 | bytes 13371904 | tf_op jit(solution)/shard_map/while/body/eval_jaxpr/sub | solution.py:107
  158.7 5.1 fusion.229
  163.9 6.8 %fusion.230 = bf16[4,64,64,8]{1,3,2,0:T(8,128)(2,1)} fusion(bf16[4,64,64,8]{1,3,2,0:T(8,128)(2,1)} %get-tuple-element.486, s32[]{:T(128)S(6)} %copy.99, bf16[4,256,64,8]{1,3,2,0:T(8,128)(2,1)S(1)} %get-tuple-element.505, f32[64,64,256]{2,1,0:T(8,128)} %fusion.229, bf16[4,64,64,256]{3,2,1,0:T(8,128)(2,1)} %get-tuple-element.510, ...), kind=kOutput, calls=%fused_computation.41.clone.1 | convolution fusion | flops 56692992 | bytes 11668992 | tf_op jit(solution)/shard_map/while/body/eval_jaxpr/hij,jhe->ihe/dot_general | solution.py:110
  170.7 3.4 fusion.232
  174.1 7.0 %fusion.231 = f32[4,256,64,8]{1,3,2,0:T(8,128)} fusion(f32[4,256,64,8]{1,3,2,0:T(8,128)} %get-tuple-element.487, s32[]{:T(128)S(6)} %copy.99, f32[64,64,256]{2,1,0:T(8,128)} %fusion.229, bf16[4,64,64,256]{3,2,1,0:T(8,128)(2,1)} %get-tuple-element.510, bf16[4,256,64,8]{1,3,2,0:T(8,128)(2,1)S(1)} %get-tuple-element.509, ...), kind=kOutput, calls=%fused_computation.37.clone.1 | convolution fusion | flops 56758528 | bytes 11931136 | tf_op jit(solution)/shard_map/while/body/eval_jaxpr/hij,ihe->jhe/dot_general | solution.py:113
  181.0 6.9 %bitcast_dynamic-update-slice_fusion.8 = bf16[4,64,64,256]{3,2,1,0:T(8,128)(2,1)} fusion(bf16[4,64,64,256]{3,2,1,0:T(8,128)(2,1)} %get-tuple-element.485, s32[]{:T(128)S(6)} %copy.99, bf16[4,64,64,256]{3,2,1,0:T(8,128)(2,1)} %get-tuple-element.510, f32[64,64,256]{2,1,0:T(8,128)} %fusion.229, bf16[4,256,64,8]{1,3,2,0:T(8,128)(2,1)S(1)} %get-tuple-element.509, ...), kind=kOutput, calls=%fused_computation.30.clone.1 | convolution fusion | flops 39850240 | bytes 13371904 | tf_op jit(solution)/shard_map/while/body/eval_jaxpr/sub | solution.py:107
  189.9 5.2 fusion.229
  195.0 6.8 %fusion.230 = bf16[4,64,64,8]{1,3,2,0:T(8,128)(2,1)} fusion(bf16[4,64,64,8]{1,3,2,0:T(8,128)(2,1)} %get-tuple-element.486, s32[]{:T(128)S(6)} %copy.99, bf16[4,256,64,8]{1,3,2,0:T(8,128)(2,1)S(1)} %get-tuple-element.505, f32[64,64,256]{2,1,0:T(8,128)} %fusion.229, bf16[4,64,64,256]{3,2,1,0:T(8,128)(2,1)} %get-tuple-element.510, ...), kind=kOutput, calls=%fused_computation.41.clone.1 | convolution fusion | flops 56692992 | bytes 11668992 | tf_op jit(solution)/shard_map/while/body/eval_jaxpr/hij,jhe->ihe/dot_general | solution.py:110
  201.8 3.4 fusion.232
  205.2 7.0 %fusion.231 = f32[4,256,64,8]{1,3,2,0:T(8,128)} fusion(f32[4,256,64,8]{1,3,2,0:T(8,128)} %get-tuple-element.487, s32[]{:T(128)S(6)} %copy.99, f32[64,64,256]{2,1,0:T(8,128)} %fusion.229, bf16[4,64,64,256]{3,2,1,0:T(8,128)(2,1)} %get-tuple-element.510, bf16[4,256,64,8]{1,3,2,0:T(8,128)(2,1)S(1)} %get-tuple-element.509, ...), kind=kOutput, calls=%fused_computation.37.clone.1 | convolution fusion | flops 56758528 | bytes 11931136 | tf_op jit(solution)/shard_map/while/body/eval_jaxpr/hij,ihe->jhe/dot_general | solution.py:113
  212.1 6.9 %bitcast_dynamic-update-slice_fusion.8 = bf16[4,64,64,256]{3,2,1,0:T(8,128)(2,1)} fusion(bf16[4,64,64,256]{3,2,1,0:T(8,128)(2,1)} %get-tuple-element.485, s32[]{:T(128)S(6)} %copy.99, bf16[4,64,64,256]{3,2,1,0:T(8,128)(2,1)} %get-tuple-element.510, f32[64,64,256]{2,1,0:T(8,128)} %fusion.229, bf16[4,256,64,8]{1,3,2,0:T(8,128)(2,1)S(1)} %get-tuple-element.509, ...), kind=kOutput, calls=%fused_computation.30.clone.1 | convolution fusion | flops 39850240 | bytes 13371904 | tf_op jit(solution)/shard_map/while/body/eval_jaxpr/sub | solution.py:107
  221.0 5.2 fusion.229
  226.1 6.8 %fusion.230 = bf16[4,64,64,8]{1,3,2,0:T(8,128)(2,1)} fusion(bf16[4,64,64,8]{1,3,2,0:T(8,128)(2,1)} %get-tuple-element.486, s32[]{:T(128)S(6)} %copy.99, bf16[4,256,64,8]{1,3,2,0:T(8,128)(2,1)S(1)} %get-tuple-element.505, f32[64,64,256]{2,1,0:T(8,128)} %fusion.229, bf16[4,64,64,256]{3,2,1,0:T(8,128)(2,1)} %get-tuple-element.510, ...), kind=kOutput, calls=%fused_computation.41.clone.1 | convolution fusion | flops 56692992 | bytes 11668992 | tf_op jit(solution)/shard_map/while/body/eval_jaxpr/hij,jhe->ihe/dot_general | solution.py:110
  232.9 3.4 fusion.232
  236.3 7.0 %fusion.231 = f32[4,256,64,8]{1,3,2,0:T(8,128)} fusion(f32[4,256,64,8]{1,3,2,0:T(8,128)} %get-tuple-element.487, s32[]{:T(128)S(6)} %copy.99, f32[64,64,256]{2,1,0:T(8,128)} %fusion.229, bf16[4,64,64,256]{3,2,1,0:T(8,128)(2,1)} %get-tuple-element.510, bf16[4,256,64,8]{1,3,2,0:T(8,128)(2,1)S(1)} %get-tuple-element.509, ...), kind=kOutput, calls=%fused_computation.37.clone.1 | convolution fusion | flops 56758528 | bytes 11931136 | tf_op jit(solution)/shard_map/while/body/eval_jaxpr/hij,ihe->jhe/dot_general | solution.py:113
  243.3 6.9 %bitcast_dynamic-update-slice_fusion.8 = bf16[4,64,64,256]{3,2,1,0:T(8,128)(2,1)} fusion(bf16[4,64,64,256]{3,2,1,0:T(8,128)(2,1)} %get-tuple-element.485, s32[]{:T(128)S(6)} %copy.99, bf16[4,64,64,256]{3,2,1,0:T(8,128)(2,1)} %get-tuple-element.510, f32[64,64,256]{2,1,0:T(8,128)} %fusion.229, bf16[4,256,64,8]{1,3,2,0:T(8,128)(2,1)S(1)} %get-tuple-element.509, ...), kind=kOutput, calls=%fused_computation.30.clone.1 | convolution fusion | flops 39850240 | bytes 13371904 | tf_op jit(solution)/shard_map/while/body/eval_jaxpr/sub | solution.py:107
  250.2 2.9 copy.67
  253.2 2.9 copy.66
  261.0 37.3 %reduce-scatter.11.cloned.1.call-done = f32[4,64,512]{2,1,0:T(8,128)} async-done(((f32[4,256,512]{2,1,0:T(8,128)}), f32[4,64,512]{2,1,0:T(8,128)}) %reduce-scatter.11.cloned.1.call-update) | async-done | bytes 524304 | tf_op jit(solution)/shard_map/reduce_scatter | solution.py:226
  300.8 43.2 %reduce-scatter.9.cloned.1.call-done = f32[4,64,512]{2,1,0:T(8,128)} async-done(((f32[4,256,512]{2,1,0:T(8,128)}), f32[4,64,512]{2,1,0:T(8,128)}) %reduce-scatter.9.cloned.1.call-update) | async-done | bytes 524304 | tf_op jit(solution)/shard_map/reduce_scatter | solution.py:220
  347.2 2.9 fusion.133
  351.5 2.8 fusion.132
  357.5 3.9 fusion.123
  361.4 21.0 %reduce-scatter.19.cloned.1.call-done = f32[64,512]{1,0:T(8,128)} async-done(((f32[512,512]{1,0:T(8,128)}), f32[64,512]{1,0:T(8,128)}) %reduce-scatter.19.cloned.1.call-update) | async-done | bytes 131088 | tf_op jit(solution)/shard_map/reduce_scatter | solution.py:276
  383.9 37.5 %reduce-scatter.13.cloned.1.call-done = f32[64,512]{1,0:T(8,128)} async-done(((f32[512,512]{1,0:T(8,128)}), f32[64,512]{1,0:T(8,128)}) %reduce-scatter.13.cloned.1.call-update) | async-done | bytes 131088 | tf_op jit(solution)/shard_map/reduce_scatter | solution.py:271
  424.1 36.4 %reduce-scatter.17.cloned.1.call-done = f32[64,512]{1,0:T(8,128)} async-done(((f32[512,512]{1,0:T(8,128)}), f32[64,512]{1,0:T(8,128)}) %reduce-scatter.17.cloned.1.call-update) | async-done | bytes 131088 | tf_op jit(solution)/shard_map/reduce_scatter | solution.py:274
  462.1 37.7 %reduce-scatter.15.cloned.1.call-done = f32[64,512]{1,0:T(8,128)} async-done(((f32[512,512]{1,0:T(8,128)}), f32[64,512]{1,0:T(8,128)}) %reduce-scatter.15.cloned.1.call-update) | async-done | bytes 131088 | tf_op jit(solution)/shard_map/reduce_scatter | solution.py:273
  501.3 53.1 %reduce-scatter.23.cloned.1.call-done = f32[256,512]{1,0:T(8,128)} async-done(((f32[2048,512]{1,0:T(8,128)}), f32[256,512]{1,0:T(8,128)}) %reduce-scatter.23.cloned.1.call-update) | async-done | bytes 524304 | tf_op jit(solution)/shard_map/reduce_scatter | solution.py:282
  554.4 1.8 convert_element_type.299
  556.2 53.3 %reduce-scatter.21.cloned.1.call-done = f32[64,2048]{1,0:T(8,128)} async-done(((f32[512,2048]{1,0:T(8,128)}), f32[64,2048]{1,0:T(8,128)}) %reduce-scatter.21.cloned.1.call-update) | async-done | bytes 524304 | tf_op jit(solution)/shard_map/reduce_scatter | solution.py:280
  609.5 1.8 convert_element_type.294
  611.3 2.6 multiply_reduce_fusion.2
  613.9 24.0 %all-reduce.9 = (bf16[512]{0:T(512)(128)(2,1)S(1)}, bf16[512]{0:T(512)(128)(2,1)S(1)}, bf16[512]{0:T(512)(128)(2,1)S(1)}, bf16[512]{0:T(512)(128)(2,1)S(1)}, bf1...) all-reduce(f32[512]{0:T(512)S(1)} %get-tuple-element.213, ...), channel_id=4, replica_groups=mesh['batch'=8,'rows'=4] {'batch'}, use_global_device_ids=true, to_apply=%region_18.19.clone | all-reduce | flops 6144 | bytes 36864
  638.6 12.2 %all-reduce.10 = (bf16[64]{0:T(256)(128)(2,1)S(1)}, bf16[64]{0:T(256)(128)(2,1)S(1)}, bf16[64]{0:T(256)(128)(2,1)S(1)}, bf16[64]{0:T(256)(128)(2,1)S(1)}, bf16[6...) all-reduce(bf16[64]{0:T(256)(128)(2,1)S(1)} %dynamic-slice.35, ...), channel_id=1, replica_groups=mesh['batch'=8,'rows'=4] {'rows'}, use_global_device_ids=true, to_apply=%region_19.20 | all-reduce | flops 768 | bytes 3072 | tf_op jit(solution)/shard_map/psum | solution.py:302
  655.5 2.0 add_convert_fusion
  657.4 2.0 all-reduce.14.cloned.1.call-done
  665.4 1.8 convert_element_type.295
  667.2 1.8 convert_element_type.300
  (231 shorter events, 83.6 us)
Async XLA Ops:
  7.2 105.1 %copy-start = (bf16[512,2048]{1,0:T(8,128)(2,1)S(1)}, bf16[512,2048]{1,0:T(8,128)(2,1)}, u32[]{:S(2)}) copy-start(bf16[512,2048]{1,0:T(8,128)(2,1)} %param.38) | copy-start | bytes 6291460
  7.2 13.5 %copy-start.5 = (bf16[4,64,512]{2,1,0:T(8,128)(2,1)S(1)}, bf16[4,64,512]{2,1,0:T(8,128)(2,1)}, u32[]{:S(2)}) copy-start(bf16[4,64,512]{2,1,0:T(8,128)(2,1)} %param.24) | copy-start | bytes 786436
  7.2 12.3 %copy-start.20 = (bf16[512,512]{1,0:T(8,128)(2,1)S(1)}, bf16[512,512]{1,0:T(8,128)(2,1)}, u32[]{:S(2)}) copy-start(bf16[512,512]{1,0:T(8,128)(2,1)} %param.31) | copy-start | bytes 1572868
  7.2 14.1 %copy-start.39 = (bf16[512]{0:T(512)(128)(2,1)S(1)}, bf16[512]{0:T(512)(128)(2,1)}, u32[]{:S(2)}) copy-start(bf16[512]{0:T(512)(128)(2,1)} %param.36) | copy-start | bytes 3076
  7.2 14.1 %copy-start.40 = (bf16[512]{0:T(512)(128)(2,1)S(1)}, bf16[512]{0:T(512)(128)(2,1)}, u32[]{:S(2)}) copy-start(bf16[512]{0:T(512)(128)(2,1)} %param.37) | copy-start | bytes 3076
  7.3 48.5 %all-gather.2.cloned.1.call-start = ((), (), s32[]{:S(2)}) async-start(), calls=%async_computation.8 | async-start | bytes 1310720 | tf_op jit(solution)/shard_map/all_gather | solution.py:159
  12.9 6.6 copy-start.6
  14.4 34.3 %collective-permute-start.2 = (bf16[4,64,512]{2,1,0:T(8,128)(2,1)S(1)}, bf16[4,64,512]{2,1,0:T(8,128)(2,1)}, u32[]{:S(2)}, u32[]{:S(2)}) collective-permute-start(bf16[4,64,512]{2,1,0:T(8,128)(2,1)S(1)} %fusion.125), channel_id=1, source_target_pairs={{0,3},{1,0},{2,1},{3,2},{4,7},{5,4},{6,5},{7,6},{8,11},{9,8},{10,9... | collective-permute-start | bytes 786440 | tf_op jit(solution)/shard_map/ppermute | solution.py:19
  19.5 12.2 %collective-permute-start = (bf16[4,64,512]{2,1,0:T(8,128)(2,1)S(1)}, bf16[4,64,512]{2,1,0:T(8,128)(2,1)}, u32[]{:S(2)}, u32[]{:S(2)}) collective-permute-start(bf16[4,64,512]{2,1,0:T(8,128)(2,1)S(1)} %fusion.125), channel_id=1, source_target_pairs={{0,1},{1,2},{2,3},{3,0},{4,5},{5,6},{6,7},{7,4},{8,9},{9,10},{10,1... | collective-permute-start | bytes 786440 | tf_op jit(solution)/shard_map/ppermute | solution.py:17
  20.5 13.7 %copy-start.12 = (bf16[4,64,512]{2,1,0:T(8,128)(2,1)S(1)}, bf16[4,64,512]{2,1,0:T(8,128)(2,1)}, u32[]{:S(2)}) copy-start(bf16[4,64,512]{2,1,0:T(8,128)(2,1)} %param.42) | copy-start | bytes 786436
  20.5 277.7 %reduce-scatter.11.cloned.1.call-start = ((), (), s32[]{:S(2)}) async-start(), calls=%async_computation.10 | async-start | bytes 2621440 | tf_op jit(solution)/shard_map/reduce_scatter | solution.py:226
  20.7 0.6 copy-start.31
  20.8 0.6 copy-start.33
  31.7 16.0 %collective-permute-start.1 = (bf16[4,64,512]{2,1,0:T(8,128)(2,1)}, bf16[4,64,512]{2,1,0:T(8,128)(2,1)S(1)}, u32[]{:S(2)}, u32[]{:S(2)}) collective-permute-start(bf16[4,64,512]{2,1,0:T(8,128)(2,1)} %collective-permute-done), channel_id=1, source_target_pairs={{0,1},{1,2},{2,3},{3,0},{4,5},{5,6},{6,7},{7,4},{8,9},{9,10},{10,1... | collective-permute-start | bytes 786440 | tf_op jit(solution)/shard_map/ppermute | solution.py:17
  110.4 1.9 copy-start.22
  112.0 6.5 copy-start.3
  112.3 6.2 copy-start.29
  117.1 1.4 copy-start.25
  117.1 1.5 copy-start.13
  118.5 1.0 copy-start.23
  119.4 136.9 %copy-start.8 = (f32[256,512]{1,0:T(8,128)}, f32[256,512]{1,0:T(8,128)S(1)}, u32[]{:S(2)}) copy-start(f32[256,512]{1,0:T(8,128)S(1)} %get-tuple-element.290) | copy-start | bytes 1572868
  121.2 4.5 copy-start.2
  253.2 90.8 %reduce-scatter.9.cloned.1.call-start = ((), (), s32[]{:S(2)}) async-start(), calls=%async_computation.9 | async-start | bytes 2621440 | tf_op jit(solution)/shard_map/reduce_scatter | solution.py:220
  256.1 0.9 copy-start.15
  256.1 2.3 copy-start.11
  256.2 3.3 copy-start.7
  256.2 126.2 %reduce-scatter.19.cloned.1.call-start = ((), (), s32[]{:S(2)}) async-start(), calls=%async_computation.14 | async-start | bytes 1179648 | tf_op jit(solution)/shard_map/reduce_scatter | solution.py:276
  258.4 163.0 %reduce-scatter.13.cloned.1.call-start = ((), (), s32[]{:S(2)}) async-start(), calls=%async_computation.11 | async-start | bytes 1179648 | tf_op jit(solution)/shard_map/reduce_scatter | solution.py:271
  259.5 41.2 %copy-start.16 = (bf16[256,512]{0,1:T(8,128)(2,1)}, bf16[256,512]{0,1:T(8,128)(2,1)S(1)}, u32[]{:S(2)}) copy-start(bf16[256,512]{0,1:T(8,128)(2,1)S(1)} %reshape.266) | copy-start | bytes 786436
  260.9 199.6 %reduce-scatter.17.cloned.1.call-start = ((), (), s32[]{:S(2)}) async-start(), calls=%async_computation.13 | async-start | bytes 1179648 | tf_op jit(solution)/shard_map/reduce_scatter | solution.py:274
  299.4 1.3 copy-start.27
  300.7 46.4 %copy-start.10 = (f32[256,2048]{1,0:T(8,128)S(1)}, f32[256,2048]{1,0:T(8,128)}, u32[]{:S(2)}) copy-start(f32[256,2048]{1,0:T(8,128)} %get-tuple-element.297) | copy-start | bytes 6291460
  300.7 46.5 %copy-start.14 = (bf16[4,64,512]{2,1,0:T(8,128)(2,1)S(1)}, bf16[4,64,512]{2,1,0:T(8,128)(2,1)}, u32[]{:S(2)}) copy-start(bf16[4,64,512]{2,1,0:T(8,128)(2,1)} %param.42) | copy-start | bytes 786436
  300.7 199.0 %reduce-scatter.15.cloned.1.call-start = ((), (), s32[]{:S(2)}) async-start(), calls=%async_computation.12 | async-start | bytes 1179648 | tf_op jit(solution)/shard_map/reduce_scatter | solution.py:273
  345.1 0.7 copy-start.18
  347.1 207.3 %reduce-scatter.23.cloned.1.call-start = ((), (), s32[]{:S(2)}) async-start(), calls=%async_computation.16 | async-start | bytes 4718592 | tf_op jit(solution)/shard_map/reduce_scatter | solution.py:282
  350.1 1.0 copy-start.4
  350.1 1.4 copy-start.26
  350.1 1.4 copy-start.30
  350.1 259.4 %reduce-scatter.21.cloned.1.call-start = ((), (), s32[]{:S(2)}) async-start(), calls=%async_computation.15 | async-start | bytes 4718592 | tf_op jit(solution)/shard_map/reduce_scatter | solution.py:280
  354.2 0.7 copy-start.42
  354.2 2.5 copy-start.41
  354.2 2.9 copy-start.17
  354.3 2.9 copy-start.24
  354.3 305.1 %all-reduce.14.cloned.1.call-start = ((), (), s32[]{:S(2)}) async-start(), calls=%async_computation.17 | async-start | bytes 1572864 | tf_op jit(solution)/shard_map/psum | solution.py:304
  357.5 65.5 %copy-start.19 = (bf16[4,64,512]{2,1,0:T(8,128)(2,1)S(1)}, bf16[4,64,512]{2,1,0:T(8,128)(2,1)}, u32[]{:S(2)}) copy-start(bf16[4,64,512]{2,1,0:T(8,128)(2,1)} %copy-done.18) | copy-start | bytes 786436
  357.5 65.4 %copy-start.21 = (bf16[512,512]{1,0:T(8,128)(2,1)S(1)}, bf16[512,512]{1,0:T(8,128)(2,1)}, u32[]{:S(2)}) copy-start(bf16[512,512]{1,0:T(8,128)(2,1)} %param.31) | copy-start | bytes 1572868
  423.0 188.3 %copy-start.28 = (bf16[4,64,512]{2,1,0:T(8,128)(2,1)S(1)}, bf16[4,64,512]{2,1,0:T(8,128)(2,1)}, u32[]{:S(2)}) copy-start(bf16[4,64,512]{2,1,0:T(8,128)(2,1)} %copy-done.27) | copy-start | bytes 786436
  423.0 188.3 %copy-start.32 = (f32[256]{0:T(256)S(1)}, f32[256]{0:T(256)}, u32[]{:S(2)}) copy-start(f32[256]{0:T(256)} %copy-done.31) | copy-start | bytes 3076
  423.0 188.3 %copy-start.34 = (f32[256]{0:T(256)S(1)}, f32[256]{0:T(256)}, u32[]{:S(2)}) copy-start(f32[256]{0:T(256)} %copy-done.33) | copy-start | bytes 3076
  556.2 57.7 %copy-start.35 = (f32[512]{0:T(512)S(1)}, f32[512]{0:T(512)}, u32[]{:S(2)}) copy-start(f32[512]{0:T(512)} %get-tuple-element.289) | copy-start | bytes 6148
  556.2 57.7 %copy-start.36 = (f32[2048]{0:T(1024)S(1)}, f32[2048]{0:T(1024)}, u32[]{:S(2)}) copy-start(f32[2048]{0:T(1024)} %get-tuple-element.287) | copy-start | bytes 24580
  556.2 57.7 %copy-start.37 = (f32[512]{0:T(512)S(1)}, f32[512]{0:T(512)}, u32[]{:S(2)}) copy-start(f32[512]{0:T(512)} %get-tuple-element.211) | copy-start | bytes 6148
  556.2 57.7 %copy-start.38 = (f32[512]{0:T(512)S(1)}, f32[512]{0:T(512)}, u32[]{:S(2)}) copy-start(f32[512]{0:T(512)} %get-tuple-element.217) | copy-start | bytes 6148
  556.2 99.3 %copy-start.9 = (f32[256,512]{1,0:T(8,128)S(1)}, f32[256,512]{1,0:T(8,128)}, u32[]{:S(2)}) copy-start(f32[256,512]{1,0:T(8,128)} %copy-done.8) | copy-start | bytes 1572868
  611.3 57.7 %copy-start.1 = (bf16[512,2048]{1,0:T(8,128)(2,1)S(1)}, bf16[512,2048]{1,0:T(8,128)(2,1)}, u32[]{:S(2)}) copy-start(bf16[512,2048]{1,0:T(8,128)(2,1)} %param.38) | copy-start | bytes 6291460
Sparse Core Ops, SparseCore 0:
  20.7 35.0 all-gather.1
  253.3 44.9 reduce-scatter.10
  300.7 43.2 reduce-scatter.8
  347.0 35.3 reduce-scatter.18
  385.4 35.9 reduce-scatter.12
  424.4 36.0 reduce-scatter.16
  463.7 35.9 reduce-scatter.14
  503.1 51.2 reduce-scatter.22
  558.1 51.3 reduce-scatter.20
  613.3 46.0 all-reduce.13
